TPU v7x, 32 devices: a whole 2x2x4 slice. The times are simulated.
32 devices in a mesh: ep: 16 (over z, y, x), dp: 2 (over core).
Axes of the slice: x: 2, y: 2, z: 4, core: 2. Of those that a mesh axis runs over, the one named last changes fastest.
Arguments:
- tokens: bfloat16 [4096, 1024], P(('ep', 'dp')), may hold values from -6 to 6
- grad_out: bfloat16 [4096, 1024], P(('ep', 'dp')), may hold values from -3 to 3
- assign: int32 [4096, 2], P(('ep', 'dp')), may hold values from 0 to 15, as said below
- router_weight: bfloat16 [16, 1024], P('ep'), may hold values from -0.1875 to 0.1875
- w_gate: bfloat16 [16, 1024, 2048], P('ep', None, 'dp'), may hold values from -0.1875 to 0.1875
- w_up: bfloat16 [16, 1024, 2048], P('ep', None, 'dp'), may hold values from -0.1875 to 0.1875
- w_down: bfloat16 [16, 2048, 1024], P('ep', 'dp'), may hold values from -0.125 to 0.125
Outputs:
- grad_tokens: bfloat16 [4096, 1024], P(('ep', 'dp'))
- grad_router: float32 [16, 1024], P('ep')
- grad_gate: bfloat16 [16, 1024, 2048], P('ep', None, 'dp')
- grad_up: bfloat16 [16, 1024, 2048], P('ep', None, 'dp')
- grad_down: bfloat16 [16, 2048, 1024], P('ep', 'dp')
Inputs may be any that keep to these rules, and one draw needn't show every extreme that they name: `assign`: in each aligned block of 128 rows (the rows of one device) the two experts of a row differ and no expert is named by more than 24 entries; in every block one expert, the same for all blocks, is named by exactly 24 entries.
All inputs are finite; a program needn't handle non-finite values.
Results may differ from a plain program's by a relative error of at most 0.007.
Values may be sent and summed in bfloat16 or wider, within the bound.
A program may use at most 192 MiB of HBM per device.

v0:
```python
import jax
import jax.numpy as jnp
from jax import lax
from jax.sharding import PartitionSpec as P


def entry_slots(assign, experts, cap):
    flat = assign.reshape(-1)
    marks = (flat[:, None] == jnp.arange(experts, dtype=jnp.int32)[None, :]).astype(jnp.int32)
    before = jnp.cumsum(marks, axis=0) - marks
    ranks = jnp.sum(before * marks, axis=1)
    return flat * cap + ranks


def expert_grads(rows, upstream, gate_vals, wg, wu, wd):
    pre_a = jnp.dot(rows, wg, preferred_element_type=jnp.float32)
    pre_b = jnp.dot(rows, wu, preferred_element_type=jnp.float32)
    sigma = jax.nn.sigmoid(pre_a)
    active = pre_a * sigma
    hidden = (active * pre_b).astype(jnp.bfloat16)
    outer = jnp.dot(hidden, wd, preferred_element_type=jnp.float32)
    up_f = upstream.astype(jnp.float32)
    grad_gates = jnp.sum(up_f * outer, axis=1)
    scaled = (gate_vals.astype(jnp.float32)[:, None] * up_f).astype(jnp.bfloat16)
    grad_hidden = jnp.dot(scaled, wd.T, preferred_element_type=jnp.float32)
    grad_a = (grad_hidden * pre_b * sigma * (1.0 + pre_a * (1.0 - sigma))).astype(jnp.bfloat16)
    grad_b = (grad_hidden * active).astype(jnp.bfloat16)
    grad_rows = jnp.dot(grad_a, wg.T, preferred_element_type=jnp.float32) + jnp.dot(
        grad_b, wu.T, preferred_element_type=jnp.float32
    )
    g_gate = jnp.dot(rows.T, grad_a, preferred_element_type=jnp.float32)
    g_up = jnp.dot(rows.T, grad_b, preferred_element_type=jnp.float32)
    g_down = jnp.dot(hidden.T, scaled, preferred_element_type=jnp.float32)
    return (grad_rows, grad_gates, g_gate, g_up, g_down)


def local(tokens, grad_out, assign, router_weight, w_gate, w_up, w_down):
    tok_rows = tokens.shape[0]
    width = tokens.shape[1]
    router_full = lax.all_gather(router_weight, "ep", axis=0, tiled=True)
    experts = router_full.shape[0]
    cap = max(2, (3 * tok_rows + experts - 1) // experts)
    choose = (assign[:, :, None] == jnp.arange(experts, dtype=jnp.int32)[None, None, :]).astype(
        jnp.float32
    )
    scores = jnp.dot(tokens, router_full.T, preferred_element_type=jnp.float32)
    picked = jnp.sum(scores[:, None, :] * choose, axis=2)
    sig = jax.nn.sigmoid(picked)
    total = jnp.sum(sig, axis=1, keepdims=True)
    gates = sig / total
    slots = entry_slots(assign, experts, cap)
    entries = 2 * tok_rows
    table = (
        jnp.full((experts * cap,), -1, dtype=jnp.int32)
        .at[slots]
        .set(jnp.arange(entries, dtype=jnp.int32))
    )
    valid = table >= 0
    safe = jnp.maximum(table, 0)
    zero_low = jnp.zeros((), jnp.bfloat16)
    send_rows = jnp.where(valid[:, None], tokens[safe // 2], zero_low).reshape(experts, cap, width)
    send_ups = jnp.where(valid[:, None], grad_out[safe // 2], zero_low).reshape(experts, cap, width)
    send_gates = (
        jnp.where(valid, gates.reshape(-1)[safe], 0.0).astype(jnp.bfloat16).reshape(experts, cap)
    )
    got_rows, got_ups, got_gates = (
        lax.all_to_all(send_rows, "ep", split_axis=0, concat_axis=0, tiled=True),
        lax.all_to_all(send_ups, "ep", split_axis=0, concat_axis=0, tiled=True),
        lax.all_to_all(send_gates, "ep", split_axis=0, concat_axis=0, tiled=True),
    )
    rows = got_rows.reshape(experts * cap, width)
    ups = got_ups.reshape(experts * cap, width)
    gts = got_gates.reshape(experts * cap)
    both_rows, both_ups, both_gates = (
        lax.all_gather(rows, "dp", axis=0, tiled=True),
        lax.all_gather(ups, "dp", axis=0, tiled=True),
        lax.all_gather(gts, "dp", axis=0, tiled=True),
    )
    part_rows, part_gates, g_gate, g_up, g_down = expert_grads(
        both_rows, both_ups, both_gates, w_gate[0], w_up[0], w_down[0]
    )
    grad_rows, grad_gates = (
        lax.psum_scatter(part_rows, "dp", scatter_dimension=0, tiled=True),
        lax.psum_scatter(part_gates, "dp", scatter_dimension=0, tiled=True),
    )
    grad_gate = g_gate.astype(jnp.bfloat16)[None]
    grad_up = g_up.astype(jnp.bfloat16)[None]
    grad_down = g_down.astype(jnp.bfloat16)[None]
    back_rows, back_gates = (
        lax.all_to_all(
            grad_rows.astype(jnp.bfloat16).reshape(experts, cap, width),
            "ep",
            split_axis=0,
            concat_axis=0,
            tiled=True,
        ),
        lax.all_to_all(
            grad_gates.astype(jnp.bfloat16).reshape(experts, cap),
            "ep",
            split_axis=0,
            concat_axis=0,
            tiled=True,
        ),
    )
    entry_rows = (
        back_rows.reshape(experts * cap, width)[slots]
        .astype(jnp.float32)
        .reshape(tok_rows, 2, width)
    )
    entry_gates = back_gates.reshape(experts * cap)[slots].astype(jnp.float32).reshape(tok_rows, 2)
    mixed = jnp.sum(gates * entry_gates, axis=1, keepdims=True)
    grad_logit = (entry_gates - mixed) / total * sig * (1.0 - sig)
    dense = jnp.sum(grad_logit[:, :, None] * choose, axis=1)
    router_term = jnp.dot(dense, router_full.astype(jnp.float32), precision=lax.Precision.HIGHEST)
    grad_tokens = (jnp.sum(entry_rows, axis=1) + router_term).astype(jnp.bfloat16)
    partial_router = jnp.dot(dense.T, tokens.astype(jnp.float32), precision=lax.Precision.HIGHEST)
    summed = lax.psum(partial_router, ("ep", "dp"))
    grad_router = lax.dynamic_slice_in_dim(summed, lax.axis_index("ep"), 1, 0)
    return (grad_tokens, grad_router, grad_gate, grad_up, grad_down)


def solution(mesh):
    return jax.shard_map(
        local,
        mesh=mesh,
        in_specs=(
            P(("ep", "dp"), None),
            P(("ep", "dp"), None),
            P(("ep", "dp"), None),
            P("ep", None),
            P("ep", None, "dp"),
            P("ep", None, "dp"),
            P("ep", "dp", None),
        ),
        out_specs=(
            P(("ep", "dp"), None),
            P("ep", None),
            P("ep", None, "dp"),
            P("ep", None, "dp"),
            P("ep", "dp", None),
        ),
        check_vma=False,
    )
```

profile of v0, /device:TPU:0, one launch (start us, length us, event | category | flops | bytes accessed | tf_op | source)
XLA Modules:
  0.0 319.3 jit_solution(11369833928976403874)
XLA Ops:
  7.2 0.9 broadcast_multiply_fusion
  8.1 0.8 copy.29
  8.9 0.1 eq.38
  9.0 0.1 eq.42
  9.3 0.1 mul.86
  9.4 0.6 reduce-window.6
  10.0 0.2 slice_reduce_fusion
  10.4 1.4 scatter_custom_fusion
  11.9 2.1 gather_fusion.1
  14.0 2.7 gather_fusion.2
  16.7 2.2 broadcast_select_fusion.1
  18.9 29.6 %all_to_all.35 = bf16[16,24,1024]{2,1,0:T(8,128)(2,1)} all-to-all(bf16[16,24,1024]{2,1,0:T(8,128)(2,1)S(1)} %get-tuple-element.14), channel_id=1, replica_groups=mesh['ep'=16,'dp'=2] {'ep'}, dimensions={0} | all-to-all | bytes 1572864 | tf_op jit(solution)/shard_map/all_to_all | solution.py:67
  48.6 3.6 %all-to-all-start.1 = ((bf16[16,24,1024]{2,1,0:T(8,128)(2,1)}), bf16[16,24,1024]{2,1,0:T(8,128)(2,1)S(1)}, u32[]{:S(2)}, u32[]{:S(2)}) async-start(bf16[16,24,1024]{2,1,0:T(8,128)(2,1)} %get-tuple-element.13), calls=%async_computation.1 | async-start | bytes 1572864 | tf_op jit(solution)/shard_map/all_to_all | solution.py:68
  52.3 46.1 %all-gather = bf16[16,1,1024]{2,1,0:T(2,128)(2,1)S(1)} all-gather(bf16[1,1,1024]{2,1,0:T(2,128)(2,1)S(1)} %bitcast.83), channel_id=1, replica_groups=mesh['ep'=16,'dp'=2] {'ep'}, dimensions={0}, use_global_device_ids=true | all-gather | bytes 34816 | tf_op jit(solution)/shard_map/all_gather | solution.py:40
  98.3 0.2 fusion.24
  98.5 0.9 copy-done.3
  99.5 0.6 dynamic-slice
  100.8 4.0 %fusion.5 = f32[768,1024]{1,0:T(8,128)S(1)} fusion(bf16[768,1024]{1,0:T(8,128)(2,1)} %all-gather.7.cloned.1.call-done, bf16[1,1024,1024]{2,1,0:T(8,128)(2,1)} %param.11), kind=kOutput, calls=%fused_computation.17 | convolution fusion | flops 1610612736 | bytes 6815744 | tf_op jit(solution)/shard_map/dot_general | solution.py:16
  104.8 1.7 copy-done.11
  106.4 4.2 %multiply_convert_fusion = (bf16[768,1024]{1,0:T(8,128)(2,1)}, f32[768,1024]{1,0:T(8,128)}) fusion(f32[768,1024]{1,0:T(8,128)S(1)} %fusion.5, bf16[768,1024]{1,0:T(8,128)(2,1)S(1)} %copy-done.7, bf16[1,1024,1024]{2,1,0:T(8,128)(2,1)S(1)} %copy-done), kind=kOutput, calls=%fused_computation.10 | convolution fusion | flops 1615331328 | bytes 11534336 | tf_op jit(solution)/shard_map/dot_general | solution.py:17
  110.6 4.4 %fusion.1 = f32[768]{0:T(1024)S(1)} fusion(bf16[768,1024]{1,0:T(8,128)(2,1)} %all-gather.5.cloned.1.call-done, bf16[768,1024]{1,0:T(8,128)(2,1)} %get-tuple-element.15, bf16[1,1024,1024]{2,1,0:T(8,128)(2,1)} %param.13), kind=kOutput, calls=%fused_computation.9 | convolution fusion | flops 1612971264 | bytes 5245952 | tf_op jit(solution)/shard_map/dot_general | solution.py:21
  115.0 2.5 all-reduce
  117.5 0.7 all_to_all.29
  118.2 3.5 %all-to-all-start.4 = ((bf16[16,1,24]{2,1,0:T(2,128)(2,1)}), bf16[16,1,24]{2,1,0:T(2,128)(2,1)S(1)}, u32[]{:S(2)}, u32[]{:S(2)}) async-start(bf16[16,1,24]{2,1,0:T(2,128)(2,1)} %all_to_all.29), calls=%async_computation.5 | async-start | bytes 16384 | tf_op jit(solution)/shard_map/all_to_all | solution.py:97
  121.8 7.1 %all-to-all-done.4 = bf16[16,1,24]{2,1,0:T(2,128)(2,1)S(1)} async-done(((bf16[16,1,24]{2,1,0:T(2,128)(2,1)}), bf16[16,1,24]{2,1,0:T(2,128)(2,1)S(1)}, u32[]{:S(2)}, u32[]{:S(2)}) %all-to-all-start.4) | async-done | bytes 800 | tf_op jit(solution)/shard_map/all_to_all | solution.py:97
  129.1 1.9 gather_fusion.4
  131.2 0.1 copy.32
  131.4 0.2 reshape.173
  131.6 2.7 gather_fusion
  134.4 9.9 %all_to_all.36 = bf16[16,1,24]{2,1,0:T(2,128)(2,1)S(1)} all-to-all(bf16[16,1,24]{2,1,0:T(2,128)(2,1)S(1)} %all_to_all.28), channel_id=1, replica_groups=mesh['ep'=16,'dp'=2] {'ep'}, dimensions={0} | all-to-all | bytes 1536 | tf_op jit(solution)/shard_map/all_to_all | solution.py:69
  144.4 2.0 all-gather.1
  146.4 6.7 %multiply_convert_fusion.1 = (bf16[768,1024]{1,0:T(8,128)(2,1)S(1)}, bf16[768,1024]{1,0:T(8,128)(2,1)S(1)}) fusion(f32[768,1024]{1,0:T(8,128)} %copy-done.11, f32[768,1024]{1,0:T(8,128)} %get-tuple-element.16, bf16[1,1024,1024]{2,1,0:T(8,128)(2,1)} %param.13, bf16[768,1024]{1,0:T(8,128)(2,1)} %all-gather.5.cloned.1.call-done, f32[768]{0:T(1024)S(1)} %reshape.231), kind=kOutput, calls=%fused_computation.11 | convolution fusion | flops 1623195648 | bytes 13110272 | tf_op jit(solution)/shard_map/dot_general | solution.py:25
  153.2 1.8 fusion.3
  155.1 3.5 %fusion.15 = f32[768,1024]{1,0:T(8,128)} fusion(f32[768,1024]{1,0:T(8,128)S(1)} %fusion.3, bf16[768,1024]{1,0:T(8,128)(2,1)S(1)} %get-tuple-element.9, bf16[1,1024,1024]{2,1,0:T(8,128)(2,1)S(1)} %copy-done), kind=kOutput, calls=%fused_computation.30 | convolution fusion | flops 1611399168 | bytes 9961472 | tf_op jit(solution)/shard_map/dot_general | solution.py:28
  158.7 7.7 %reduce-scatter.2.cloned.1.call-done = f32[384,1024]{1,0:T(8,128)} async-done(((f32[768,1024]{1,0:T(8,128)}), f32[384,1024]{1,0:T(8,128)}) %reduce-scatter.2.cloned.1.call-update) | async-done | bytes 1572880 | tf_op jit(solution)/shard_map/reduce_scatter | solution.py:83
  166.3 2.4 convert_element_type.75
  168.7 6.9 %all-to-all-start.3 = ((bf16[16,24,1024]{2,1,0:T(8,128)(2,1)}), bf16[16,24,1024]{2,1,0:T(8,128)(2,1)S(1)}, u32[]{:S(2)}, u32[]{:S(2)}) async-start(bf16[16,24,1024]{2,1,0:T(8,128)(2,1)} %bitcast.80), calls=%async_computation.4 | async-start | bytes 1572864 | tf_op jit(solution)/shard_map/all_to_all | solution.py:90
  175.6 0.3 all-reduce.3.cloned.1.call-start
  175.9 0.9 fusion.37
  176.8 5.2 %convert_bitcast_fusion.2 = bf16[1,1024,1024]{2,1,0:T(8,128)(2,1)} fusion(bf16[768,1024]{1,0:T(8,128)(2,1)} %all-gather.7.cloned.1.call-done, bf16[768,1024]{1,0:T(8,128)(2,1)} %copy-done.14), kind=kOutput, calls=%fused_computation.29 | convolution fusion | flops 1611661312 | bytes 5242880 | tf_op jit(solution)/shard_map/dot_general | solution.py:31
  182.0 3.3 %convert_bitcast_fusion = bf16[1,1024,1024]{2,1,0:T(8,128)(2,1)} fusion(bf16[768,1024]{1,0:T(8,128)(2,1)S(1)} %copy-done.15, bf16[768,1024]{1,0:T(8,128)(2,1)S(1)} %copy-done.9, f32[768]{0:T(1024)S(1)} %reshape.231), kind=kOutput, calls=%fused_computation.27 | convolution fusion | flops 1614020608 | bytes 5245952 | tf_op jit(solution)/shard_map/dot_general | solution.py:33
  185.3 3.2 convert_bitcast_fusion.1
  188.5 115.0 %all-reduce.3.cloned.1.call-done = f32[16,1024]{1,0:T(8,128)} async-done(((f32[16,1024]{1,0:T(8,128)}), f32[16,1024]{1,0:T(8,128)}) %all-reduce.3.cloned.1.call-update) | async-done | bytes 65552 | tf_op jit(solution)/shard_map/psum | solution.py:117
  303.4 1.4 constant_dynamic-slice_fusion
  304.8 2.0 gather_fusion.3
  306.7 1.7 reshape.174
  308.4 2.1 reduce_sum.69
  310.6 2.2 fusion.20
  (69 shorter events, 1.4 us)
Async XLA Ops:
  7.2 99.2 %copy-start = (bf16[1,1024,1024]{2,1,0:T(8,128)(2,1)S(1)}, bf16[1,1024,1024]{2,1,0:T(8,128)(2,1)}, u32[]{:S(2)}) copy-start(bf16[1,1024,1024]{2,1,0:T(8,128)(2,1)} %param.12) | copy-start | bytes 6291460
  7.2 4.7 %copy-start.2 = (bf16[128,1024]{1,0:T(8,128)(2,1)S(1)}, bf16[128,1024]{1,0:T(8,128)(2,1)}, u32[]{:S(2)}) copy-start(bf16[128,1024]{1,0:T(8,128)(2,1)} %param.8) | copy-start | bytes 786436
  7.2 93.6 %all-gather.7.cloned.1.call-start = ((), (), s32[]{:S(2)}) async-start(), calls=%async_computation.7 | async-start | bytes 2359296 | tf_op jit(solution)/shard_map/all_gather | solution.py:75
  11.9 2.1 copy-start.1
  18.9 33.4 %copy-start.5 = (bf16[1,1024]{1,0:T(2,128)(2,1)S(1)}, bf16[1,1024]{1,0:T(2,128)(2,1)}, u32[]{:S(2)}) copy-start(bf16[1,1024]{1,0:T(2,128)(2,1)} %param.10) | copy-start | bytes 6148
  48.5 50.9 %copy-start.4 = (s32[128,2]{0,1:T(2,128)S(1)}, s32[128,2]{0,1:T(2,128)}, u32[]{:S(2)}) copy-start(s32[128,2]{0,1:T(2,128)} %param.9) | copy-start | bytes 3076
  48.5 50.9 %copy-start.10 = (u32[32]{0:T(128)S(1)}, u32[32]{0:T(128)}, u32[]{:S(2)}) copy-start(u32[32]{0:T(128)} %constant.57) | copy-start | bytes 388
  48.6 50.0 %all-to-all-start.1 = ((bf16[16,24,1024]{2,1,0:T(8,128)(2,1)}), bf16[16,24,1024]{2,1,0:T(8,128)(2,1)S(1)}, u32[]{:S(2)}, u32[]{:S(2)}) async-start(bf16[16,24,1024]{2,1,0:T(8,128)(2,1)} %get-tuple-element.13), calls=%async_computation.1 | async-start | bytes 1572864 | tf_op jit(solution)/shard_map/all_to_all | solution.py:68
  52.2 58.4 %all-gather.5.cloned.1.call-start = ((), (), s32[]{:S(2)}) async-start(), calls=%async_computation.6 | async-start | bytes 2359296 | tf_op jit(solution)/shard_map/all_gather | solution.py:76
  98.5 0.9 copy-start.3
  100.8 5.7 %copy-start.7 = (bf16[768,1024]{1,0:T(8,128)(2,1)S(1)}, bf16[768,1024]{1,0:T(8,128)(2,1)}, u32[]{:S(2)}) copy-start(bf16[768,1024]{1,0:T(8,128)(2,1)} %all-gather.7.cloned.1.call-done) | copy-start | bytes 4718596
  104.7 1.7 copy-start.11
  118.2 10.7 %all-to-all-start.4 = ((bf16[16,1,24]{2,1,0:T(2,128)(2,1)}), bf16[16,1,24]{2,1,0:T(2,128)(2,1)S(1)}, u32[]{:S(2)}, u32[]{:S(2)}) async-start(bf16[16,1,24]{2,1,0:T(2,128)(2,1)} %all_to_all.29), calls=%async_computation.5 | async-start | bytes 16384 | tf_op jit(solution)/shard_map/all_to_all | solution.py:97
  121.7 44.6 %reduce-scatter.2.cloned.1.call-start = ((), (), s32[]{:S(2)}) async-start(), calls=%async_computation.8 | async-start | bytes 4718592 | tf_op jit(solution)/shard_map/reduce_scatter | solution.py:83
  146.4 6.8 %copy-start.6 = (bf16[1,1024,1024]{2,1,0:T(8,128)(2,1)S(1)}, bf16[1,1024,1024]{2,1,0:T(8,128)(2,1)}, u32[]{:S(2)}) copy-start(bf16[1,1024,1024]{2,1,0:T(8,128)(2,1)} %param.11) | copy-start | bytes 6291460
  153.2 1.9 copy-start.14
  153.2 1.9 copy-start.12
  168.7 136.1 %all-to-all-start.3 = ((bf16[16,24,1024]{2,1,0:T(8,128)(2,1)}), bf16[16,24,1024]{2,1,0:T(8,128)(2,1)S(1)}, u32[]{:S(2)}, u32[]{:S(2)}) async-start(bf16[16,24,1024]{2,1,0:T(8,128)(2,1)} %bitcast.80), calls=%async_computation.4 | async-start | bytes 1572864 | tf_op jit(solution)/shard_map/all_to_all | solution.py:90
  175.6 127.8 %all-reduce.3.cloned.1.call-start = ((), (), s32[]{:S(2)}) async-start(), calls=%async_computation.9 | async-start | bytes 131072 | tf_op jit(solution)/shard_map/psum | solution.py:117
  176.8 5.2 %copy-start.9 = (bf16[768,1024]{1,0:T(8,128)(2,1)S(1)}, bf16[768,1024]{1,0:T(8,128)(2,1)}, u32[]{:S(2)}) copy-start(bf16[768,1024]{1,0:T(8,128)(2,1)} %all-gather.5.cloned.1.call-done) | copy-start | bytes 4718596
  176.8 5.2 %copy-start.15 = (bf16[768,1024]{1,0:T(8,128)(2,1)S(1)}, bf16[768,1024]{1,0:T(8,128)(2,1)}, u32[]{:S(2)}) copy-start(bf16[768,1024]{1,0:T(8,128)(2,1)} %get-tuple-element.15) | copy-start | bytes 4718596
  182.0 3.3 %copy-start.8 = (bf16[768,1024]{1,0:T(8,128)(2,1)S(1)}, bf16[768,1024]{1,0:T(8,128)(2,1)}, u32[]{:S(2)}) copy-start(bf16[768,1024]{1,0:T(8,128)(2,1)} %all-gather.7.cloned.1.call-done) | copy-start | bytes 4718596
  182.0 3.3 %copy-start.13 = (bf16[768,1024]{1,0:T(8,128)(2,1)S(1)}, bf16[768,1024]{1,0:T(8,128)(2,1)}, u32[]{:S(2)}) copy-start(bf16[768,1024]{1,0:T(8,128)(2,1)} %copy-done.12) | copy-start | bytes 4718596
Sparse Core Ops, SparseCore 0:
  48.7 7.5 all-gather.6
  99.6 7.4 all-gather.4
  158.7 7.5 reduce-scatter.1
  182.3 121.1 all-reduce.2
where the time goes:
time: 321 us; the launch traced here: 319 us
  waiting for transfers between devices  130 us (40%)
  blocking collectives  90.1 us (28%)
  matrix products  39.5 us (12%)
  local copies, waits for them, and re-layouts  22.1 us (7%)
  between operations  14.8 us (5%)
  starting transfers between devices  14.4 us (4%)
  other arithmetic  8.53 us (3%)
    psum x1, waiting for transfers between devices, local(): summed = lax.psum(partial_router, ('ep', 'dp'))  115 us
    all_gather x1, blocking collectives, local(): router_full = lax.all_gather(router_weight, 'ep', axis=0, tiled=True)  46.1 us
    all_to_all x1, blocking collectives, local(): lax.all_to_all(send_rows, 'ep', split_axis=0, concat_axis=0, tiled=True)  29.6 us
    all_to_all x1, blocking collectives, local(): lax.all_to_all(send_gates, 'ep', split_axis=0, concat_axis=0, tiled=True)  9.88 us
    reduce_scatter x1, waiting for transfers between devices, local(): lax.psum_scatter(part_rows, 'dp', scatter_dimension=0, tiled=True)  7.66 us
    all_to_all x1, waiting for transfers between devices, local(): lax.all_to_all(grad_gates.astype(jnp.bfloat16).reshape(experts, cap), 'ep...  7.13 us
    all_to_all x1, starting transfers between devices, local(): lax.all_to_all(grad_rows.astype(jnp.bfloat16).reshape(experts, cap, width...  6.88 us
    dot_general x1, matrix products, expert_grads(): grad_hidden = jnp.dot(scaled, wd.T, preferred_element_type=jnp.float32)  6.74 us
  transfers between devices with their start and end apart: 7, of which 3 were waited for; matrix products, arithmetic and copies ran while one was open for 7% of the time, Pallas kernels for 0%

commit v1 on v0

v1 whole, which is shorter than its diff:
```python
import functools

import jax
import jax.numpy as jnp
from jax import lax
from jax.experimental import pallas as pl
from jax.experimental.pallas import tpu as pltpu
from jax.sharding import PartitionSpec as P

LANES = 128
SUB = 8
MESH = pl.DeviceIdType.MESH


def remote(src, dst, send, recv, where):
    return pltpu.make_async_remote_copy(
        src_ref=src, dst_ref=dst, send_sem=send, recv_sem=recv, device_id=where, device_id_type=MESH
    )


def greet(n, me, half, both):
    barrier = pltpu.get_barrier_semaphore()

    def step(k, c):
        other = lax.rem(me + k, n)
        pl.semaphore_signal(barrier, inc=1, device_id=(other, half), device_id_type=MESH)
        if both:
            pl.semaphore_signal(barrier, inc=1, device_id=(other, 1 - half), device_id_type=MESH)
        return c

    lax.fori_loop(1, n, step, 0)
    pl.semaphore_signal(barrier, inc=1, device_id=(me, 1 - half), device_id_type=MESH)
    pl.semaphore_wait(barrier, 2 * n - 1 if both else n)


def gather_kernel(n, mine, out, local, send, recv):
    me, half = lax.axis_index("ep"), lax.axis_index("dp")
    own = pltpu.make_async_copy(mine, out.at[me], local)
    own.start()
    greet(n, me, half, False)

    def push(k, c):
        other = lax.rem(me + n - k, n)
        remote(mine, out.at[me], send.at[k], recv.at[k], (other, half)).start()
        return c

    lax.fori_loop(1, n, push, 0)

    def done(k, c):
        source = lax.rem(me + k, n)
        remote(mine, out.at[source], send.at[k], recv.at[k], (source, half)).wait()
        return c

    lax.fori_loop(1, n, done, 0)
    own.wait()


def dispatch_kernel(n, x, g, xa, ga, local, sx, rx, sg, rg, fx, ax, fg, ag):
    me, half = lax.axis_index("ep"), lax.axis_index("dp")
    partner = (me, 1 - half)
    own = pltpu.make_async_copy(x.at[me], xa.at[half, me], local.at[0])
    own_g = pltpu.make_async_copy(g.at[me], ga.at[half, me], local.at[1])
    own.start()
    own_g.start()
    greet(n, me, half, False)

    def push(k, c):
        other = lax.rem(me + n - k, n)
        remote(x.at[other], xa.at[half, me], sx.at[k], rx.at[k], (other, half)).start()
        remote(g.at[other], ga.at[half, me], sg.at[k], rg.at[k], (other, half)).start()
        return c

    lax.fori_loop(1, n, push, 0)
    remote(x.at[me], xa.at[half, me], fx.at[0], ax.at[0], partner).start()
    remote(g.at[me], ga.at[half, me], fg.at[0], ag.at[0], partner).start()

    def relay(k, c):
        source = lax.rem(me + k, n)
        remote(x.at[source], xa.at[half, source], sx.at[k], rx.at[k], partner).wait_recv()
        remote(xa.at[half, source], xa.at[half, source], fx.at[k], ax.at[k], partner).start()
        remote(g.at[source], ga.at[half, source], sg.at[k], rg.at[k], partner).wait_recv()
        remote(ga.at[half, source], ga.at[half, source], fg.at[k], ag.at[k], partner).start()
        return c

    lax.fori_loop(1, n, relay, 0)

    def done(k, c):
        source = lax.rem(me + k, n)
        remote(x.at[me], xa.at[1 - half, source], fx.at[k], ax.at[k], partner).wait()
        remote(g.at[me], ga.at[1 - half, source], fg.at[k], ag.at[k], partner).wait()
        return c

    lax.fori_loop(0, n, done, 0)

    def drain(k, c):
        other = lax.rem(me + n - k, n)
        remote(x.at[other], xa.at[half, me], sx.at[k], rx.at[k], partner).wait_send()
        remote(g.at[other], ga.at[half, me], sg.at[k], rg.at[k], partner).wait_send()
        return c

    lax.fori_loop(1, n, drain, 0)
    own.wait()
    own_g.wait()


def combine_kernel(n, x, g, xb, gb, xin, gin, xs, gs, local, fx, ax, fg, ag, sx, rx, sg, rg):
    me, half = lax.axis_index("ep"), lax.axis_index("dp")
    partner = (me, 1 - half)
    greet(n, me, half, False)

    def give(k, c):
        other = lax.rem(me + n - k, n)
        remote(g.at[1 - half, other], gin.at[other], fg.at[k], ag.at[k], partner).start()
        remote(x.at[1 - half, other], xin.at[other], fx.at[k], ax.at[k], partner).start()
        return c

    lax.fori_loop(0, n, give, 0)

    def add(k, other):
        remote(g.at[1 - half, other], gin.at[other], fg.at[k], ag.at[k], partner).wait()
        gs[other] = g[half, other] + gin[other]
        remote(x.at[1 - half, other], xin.at[other], fx.at[k], ax.at[k], partner).wait()
        xs[other] = (x[half, other].astype(jnp.float32) + xin[other].astype(jnp.float32)).astype(xs.dtype)

    def push(k, c):
        other = lax.rem(me + n - k, n)
        add(k, other)
        remote(gs.at[other], gb.at[me], sg.at[k], rg.at[k], (other, half)).start()
        remote(xs.at[other], xb.at[me], sx.at[k], rx.at[k], (other, half)).start()
        return c

    lax.fori_loop(1, n, push, 0)
    add(0, me)
    own_g = pltpu.make_async_copy(gs.at[me], gb.at[me], local.at[0])
    own = pltpu.make_async_copy(xs.at[me], xb.at[me], local.at[1])
    own_g.start()
    own.start()

    def done(k, c):
        source = lax.rem(me + k, n)
        remote(gs.at[source], gb.at[source], sg.at[k], rg.at[k], (source, half)).wait()
        remote(xs.at[source], xb.at[source], sx.at[k], rx.at[k], (source, half)).wait()
        return c

    lax.fori_loop(1, n, done, 0)
    own_g.wait()
    own.wait()


def router_kernel(n, mine, out, land, near, s0, r0, s1, r1):
    me, half = lax.axis_index("ep"), lax.axis_index("dp")
    greet(n, me, half, True)
    remote(mine.at[me], near.at[me], s1.at[0], r1.at[0], (me, 1 - half)).start()

    def push(k, c):
        other = lax.rem(me + n - k, n)
        remote(mine.at[other], land.at[me], s0.at[k], r0.at[k], (other, half)).start()
        remote(mine.at[other], near.at[me], s1.at[k], r1.at[k], (other, 1 - half)).start()
        return c

    lax.fori_loop(1, n, push, 0)
    remote(mine.at[me], near.at[me], s1.at[0], r1.at[0], (me, 1 - half)).wait()

    def done(k, total):
        source = lax.rem(me + k, n)
        remote(mine.at[source], land.at[source], s0.at[k], r0.at[k], (source, half)).wait()
        remote(mine.at[source], near.at[source], s1.at[k], r1.at[k], (source, 1 - half)).wait()
        return total + (land[source] + near[source])

    out[...] = lax.fori_loop(1, n, done, mine[me] + near[me])


def call(body, n, ident, out_shape, in_spaces, out_spaces, scratch, *args):
    return pl.pallas_call(
        functools.partial(body, n),
        out_shape=out_shape,
        in_specs=[pl.BlockSpec(memory_space=s) for s in in_spaces],
        out_specs=jax.tree.map(lambda s: pl.BlockSpec(memory_space=s), out_spaces),
        scratch_shapes=scratch,
        compiler_params=pltpu.CompilerParams(collective_id=ident, has_side_effects=True),
    )(*args)


def local(tokens, grad_out, assign, router_weight, w_gate, w_up, w_down):
    n = lax.axis_size("ep")
    tok, width = tokens.shape
    experts = n
    need = max(2, (3 * tok + experts - 1) // experts)
    cap = -(-need // SUB) * SUB
    f32, bf = jnp.float32, jnp.bfloat16
    dma = pltpu.SemaphoreType.DMA
    vm, hbm = pltpu.VMEM, pl.ANY
    tile = (SUB, width // SUB)

    router_full = call(
        gather_kernel, n, 0, jax.ShapeDtypeStruct((n,) + tile, f32), [vm], vm,
        [dma(()), dma((n,)), dma((n,))], router_weight.astype(f32).reshape(tile),
    ).reshape(n, width)

    marks = (assign.reshape(-1)[:, None] == jnp.arange(experts, dtype=jnp.int32)[None, :]).astype(f32)
    low = jnp.tril(jnp.ones((2 * tok, 2 * tok), f32), -1)
    before = jnp.dot(low.astype(bf), marks.astype(bf), preferred_element_type=f32)
    ranks = jnp.sum(before * marks, axis=1).astype(jnp.int32)
    slots = (assign.reshape(-1) * cap + ranks).reshape(tok, 2)
    ids = jnp.arange(experts * cap, dtype=jnp.int32)
    hit0 = slots[:, 0][None, :] == ids[:, None]
    hit1 = slots[:, 1][None, :] == ids[:, None]
    pick = (hit0 | hit1).astype(bf)
    stacked = jnp.concatenate([tokens, grad_out], axis=1)
    send = jnp.dot(pick, stacked, preferred_element_type=f32).astype(bf)
    send = send.reshape(experts, cap, 2, width).transpose(0, 2, 1, 3).reshape(experts, 2 * cap, width)

    choose = marks.reshape(tok, 2, experts)
    scores = jnp.dot(tokens, router_full.astype(bf).T, preferred_element_type=f32)
    picked = jnp.sum(scores[:, None, :] * choose, axis=2)
    sig = jax.nn.sigmoid(picked)
    total = jnp.sum(sig, axis=1, keepdims=True)
    gates = sig / total
    low_gates = gates.astype(bf).astype(f32)
    slot_gates = jnp.sum(
        jnp.where(hit0, low_gates[:, 0][None, :], 0.0) + jnp.where(hit1, low_gates[:, 1][None, :], 0.0), axis=1
    ).reshape(experts, 1, cap)
    send_gates = jnp.pad(slot_gates, ((0, 0), (0, SUB - 1), (0, LANES - cap)))

    got, got_gates = call(
        dispatch_kernel, n, 1,
        (jax.ShapeDtypeStruct((2, n, 2 * cap, width), bf), jax.ShapeDtypeStruct((2, n, SUB, LANES), f32)),
        [hbm, hbm], (hbm, hbm),
        [dma((2,))] + [dma((n,))] * 8, send, send_gates,
    )
    rows_total = 2 * n * cap
    rows = got[:, :, :cap].reshape(rows_total, width)
    ups = got[:, :, cap:].reshape(rows_total, width)
    gts = got_gates[:, :, 0, :cap].reshape(rows_total, 1)

    wg, wu, wd = w_gate[0], w_up[0], w_down[0]
    pre_a = jnp.dot(rows, wg, preferred_element_type=f32)
    pre_b = jnp.dot(rows, wu, preferred_element_type=f32)
    sigma = jax.nn.sigmoid(pre_a)
    active = pre_a * sigma
    hid = active * pre_b
    hidden = hid.astype(bf)
    lifted = jnp.dot(ups, wd.T, preferred_element_type=f32)
    part_gates = jnp.sum(hidden.astype(f32) * lifted, axis=1)
    grad_hidden = lifted * gts
    grad_a = (grad_hidden * pre_b * sigma * (1.0 + pre_a * (1.0 - sigma))).astype(bf)
    grad_b = (grad_hidden * active).astype(bf)
    part_rows = jnp.dot(grad_a, wg.T, preferred_element_type=f32) + jnp.dot(
        grad_b, wu.T, preferred_element_type=f32
    )
    scaled = (gts * ups.astype(f32)).astype(bf)

    tiles = jnp.pad(part_gates.reshape(2, n, 1, cap), ((0, 0), (0, 0), (0, SUB - 1), (0, LANES - cap)))
    back_rows, back_gates = call(
        combine_kernel, n, 2,
        (jax.ShapeDtypeStruct((n, cap, width), bf), jax.ShapeDtypeStruct((n, SUB, LANES), f32)),
        [vm, vm], (vm, vm),
        [vm((n, cap, width), bf), vm((n, SUB, LANES), f32), vm((n, cap, width), bf), vm((n, SUB, LANES), f32),
         dma((2,))] + [dma((n,))] * 8,
        part_rows.astype(bf).reshape(2, n, cap, width), tiles,
    )
    turn = (((0,), (0,)), ((), ()))
    grad_gate = lax.dot_general(rows, grad_a, turn, preferred_element_type=f32).astype(bf)[None]
    grad_up = lax.dot_general(rows, grad_b, turn, preferred_element_type=f32).astype(bf)[None]
    grad_down = lax.dot_general(hidden, scaled, turn, preferred_element_type=f32).astype(bf)[None]

    slot_back = back_gates[:, 0, :cap].reshape(1, experts * cap).astype(bf).astype(f32)
    entry0 = jnp.sum(jnp.where(hit0.T, slot_back, 0.0), axis=1)
    entry1 = jnp.sum(jnp.where(hit1.T, slot_back, 0.0), axis=1)
    entry_gates = jnp.stack([entry0, entry1], axis=1)
    mixed = jnp.sum(gates * entry_gates, axis=1, keepdims=True)
    grad_logit = (entry_gates - mixed) / total * sig * (1.0 - sig)
    dense = jnp.sum(grad_logit[:, :, None] * choose, axis=1)
    partial = jnp.dot(dense.T, tokens.astype(f32), precision=lax.Precision.HIGHEST)
    grad_router = call(
        router_kernel, n, 3, jax.ShapeDtypeStruct(tile, f32), [vm], vm,
        [vm((n,) + tile, f32), vm((n,) + tile, f32)] + [dma((n,))] * 4, partial.reshape((n,) + tile),
    ).reshape(1, width)
    entry_sum = jnp.dot(pick.T, back_rows.reshape(experts * cap, width), preferred_element_type=f32)
    router_term = jnp.dot(dense, router_full, precision=lax.Precision.HIGHEST)
    grad_tokens = (entry_sum + router_term).astype(bf)
    return (grad_tokens, grad_router, grad_gate, grad_up, grad_down)


def solution(mesh):
    return jax.shard_map(
        local,
        mesh=mesh,
        in_specs=(
            P(("ep", "dp"), None),
            P(("ep", "dp"), None),
            P(("ep", "dp"), None),
            P("ep", None),
            P("ep", None, "dp"),
            P("ep", None, "dp"),
            P("ep", "dp", None),
        ),
        out_specs=(
            P(("ep", "dp"), None),
            P("ep", None),
            P("ep", None, "dp"),
            P("ep", None, "dp"),
            P("ep", "dp", None),
        ),
        check_vma=False,
    )
```

time: 321 us -> 151 us (0.47)
  waiting for transfers between devices: 130 us -> 0 us
  Pallas kernels: 0 us -> 95.4 us
  blocking collectives: 90.1 us -> 0 us
  starting transfers between devices: 14.4 us -> 0 us
  between operations: 14.8 us -> 0.87 us
  local copies, waits for them, and re-layouts: 22.1 us -> 15.6 us
  matrix products: 39.5 us -> 34.9 us
  other arithmetic: 8.53 us -> 4.15 us
    psum x1 -> x0, waiting for transfers between devices: 115 us -> none  [local(): summed = lax.psum(partial_router, ('ep', 'dp'))]
    pallas_call x0 -> x4, Pallas kernels: none -> 95.4 us  [call(): pl.pallas_call(functools.partial(body, n), out_shape=out_shape, in_specs=...]
    all_gather x2 -> x0, blocking collectives: 48.1 us -> none  [the longest x1 46.1 us: local(): router_full = lax.all_gather(router_weight, 'ep', axis=0, tiled=True)]
    all_to_all x2 -> x0, blocking collectives: 39.5 us -> none  [the longest x1 29.6 us: local(): lax.all_to_all(send_rows, 'ep', split_axis=0, concat_axis=0, tiled=True)]
    all_to_all x3 -> x0, starting transfers between devices: 14 us -> none  [the longest x1 6.88 us: local(): lax.all_to_all(grad_rows.astype(jnp.bfloat16).reshape(experts, cap, width...]
    gather x5 -> x0, local copies, waits for them, and re-layouts: 11.3 us -> none  [the longest x1 2.7 us: local(): gates.reshape(-1)[safe]]
    reduce_scatter x1 -> x0, waiting for transfers between devices: 7.66 us -> none  [local(): lax.psum_scatter(part_rows, 'dp', scatter_dimension=0, tiled=True)]
    all_to_all x3 -> x0, waiting for transfers between devices: 7.14 us -> none  [the longest x1 7.13 us: local(): lax.all_to_all(grad_gates.astype(jnp.bfloat16).reshape(experts, cap), 'ep...]
  transfers between devices with their start and end apart: 7 -> 0, of which waited for: 3 -> 0; matrix products, arithmetic and copies ran while one was open for 7% -> 0% of each run, Pallas kernels for 0% -> 0%
where the time goes in v1:
time: 151 us
  Pallas kernels  95.4 us (63%)
  matrix products  34.9 us (23%)
  local copies, waits for them, and re-layouts  15.6 us (10%)
  other arithmetic  4.15 us (3%)
    pallas_call x4, Pallas kernels, call(): pl.pallas_call(functools.partial(body, n), out_shape=out_shape, in_specs=...  95.4 us
    reshape x2, local copies, waits for them, and re-layouts, local(): send.reshape(experts, cap, 2, width).transpose(0, 2, 1, 3)  6.83 us
    dot_general x1, matrix products, local(): lifted = jnp.dot(ups, wd.T, preferred_element_type=f32)  6.22 us
    slice x1, local copies, waits for them, and re-layouts, local(): ups = got[:, :, cap:].reshape(rows_total, width)  3.52 us
    dot_general x1, matrix products, local(): pre_a = jnp.dot(rows, wg, preferred_element_type=f32)  3.5 us
    dot_general x1, matrix products, local(): pre_b = jnp.dot(rows, wu, preferred_element_type=f32)  3.46 us
    dot_general x1, matrix products, local(): lax.dot_general(hidden, scaled, turn, preferred_element_type=f32).astype(bf)  3.25 us
    dot_general x1, matrix products, local(): lax.dot_general(rows, grad_a, turn, preferred_element_type=f32).astype(bf)  3.18 us

profile of v1, /device:TPU:0, one launch (start us, length us, event | category | flops | bytes accessed | tf_op | source)
XLA Modules:
  0.0 150.9 jit_solution(15875856060401608010)
XLA Ops:
  0.6 0.0 copy-start
  0.6 1.4 reshape.147
  2.1 11.4 %shard_map.110 = f32[16,8,128]{2,1,0:T(8,128)} custom-call(f32[8,128]{1,0:T(8,128)} %bitcast.81), custom_call_target="tpu_custom_call" | custom-call | tf_op jit(solution)/shard_map/pallas_call | solution.py:174
  13.5 1.1 fusion.32
  14.6 0.7 select_reduce_fusion.3
  15.4 0.8 copy.42
  16.2 0.1 eq.66
  16.3 0.3 fusion.15
  16.6 0.1 convert_element_type.91
  16.8 0.1 copy.43
  16.8 0.7 multiply_add_fusion
  17.5 0.1 add_reduce_fusion
  17.7 0.1 reshape.140
  17.8 0.6 pad.8.g
  18.4 2.7 %convolution_convert_fusion = bf16[384,2048]{1,0:T(8,128)(2,1)} fusion(bf16[128,1024]{1,0:T(8,128)(2,1)} %param.8, bf16[128,1024]{1,0:T(8,128)(2,1)} %param.7, s32[128]{0:T(128)S(1)} %get-tuple-element.28, s32[128]{0:T(128)S(1)} %get-tuple-element.27), kind=kOutput, calls=%fused_computation.8 | convolution fusion | flops 203309056 | bytes 2098176 | tf_op jit(solution)/shard_map/dot_general | solution.py:210
  21.2 3.8 %reshape.135 = bf16[16,24,2,1024]{3,2,1,0:T(2,128)(2,1)} reshape(bf16[384,2048]{1,0:T(8,128)(2,1)} %convolution_convert_fusion) | data formatting | bytes 3145728 | tf_op jit(solution)/shard_map/reshape | solution.py:211
  25.0 3.0 %copy.44 = bf16[16,24,2,1024]{3,1,2,0:T(8,128)(2,1)} copy(bf16[16,24,2,1024]{3,2,1,0:T(2,128)(2,1)} %reshape.135) | data formatting | bytes 3145728 | tf_op jit(solution)/shard_map/reshape | solution.py:211
  28.0 44.1 %shard_map.111 = (bf16[2,16,48,1024]{3,2,1,0:T(8,128)(2,1)}, f32[2,16,8,128]{3,2,1,0:T(8,128)}) custom-call(bf16[16,48,1024]{2,1,0:T(8,128)(2,1)} %bitcast.67, f32[16,8,128]{2,1,0:T(8,128)} %pad.8.g), custom_call_target="tpu_custom_call" | custom-call | tf_op jit(solution)/shard_map/pallas_call | solution.py:174
  72.1 0.0 copy-start.8
  72.1 3.5 %fusion.43 = (bf16[2,16,24,1024]{3,2,1,0:T(8,128)(2,1)}, bf16[2,16,24,1024]{3,2,1,0:T(8,128)(2,1)S(1)}) fusion(bf16[2,16,48,1024]{3,2,1,0:T(8,128)(2,1)} %get-tuple-element.9), kind=kLoop, calls=%fused_computation.82 | loop fusion | bytes 6291456 | tf_op jit(solution)/shard_map/slice | solution.py:233
  75.6 0.0 copy-done.8
  75.6 3.5 %fusion.3 = f32[768,1024]{1,0:T(8,128)} fusion(bf16[768,1024]{1,0:T(8,128)(2,1)S(1)} %bitcast.70, bf16[1,1024,1024]{2,1,0:T(8,128)(2,1)S(1)} %copy-done.8), kind=kOutput, calls=%fused_computation.11 | convolution fusion | flops 1610612736 | bytes 6815744 | tf_op jit(solution)/shard_map/dot_general | solution.py:237
  79.1 3.5 %fusion.7 = f32[768,1024]{1,0:T(8,128)} fusion(bf16[768,1024]{1,0:T(8,128)(2,1)S(1)} %bitcast.71, bf16[1,1024,1024]{2,1,0:T(8,128)(2,1)S(1)} %copy-done.10), kind=kOutput, calls=%fused_computation.15 | convolution fusion | flops 1610612736 | bytes 6815744 | tf_op jit(solution)/shard_map/dot_general | solution.py:238
  82.6 0.9 slice_reduce_fusion
  83.6 0.1 mul.88
  83.7 0.0 copy-start.4
  83.7 6.2 %multiply_reduce_fusion = (f32[768]{0:T(1024)S(1)}, bf16[768,1024]{1,0:T(8,128)(2,1)S(1)}, bf16[768,1024]{1,0:T(8,128)(2,1)S(1)}, bf16[768,1024]{1,0:T(8,128)(2,1)S(1)}) fusion(f32[768,1024]{1,0:T(8,128)} %fusion.7, f32[768,1024]{1,0:T(8,128)} %fusion.3, f32[768]{0:T(1024)S(1)} %mul.88, bf16[768,1024]{1,0:T(8,128)(2,1)} %bitcast.74, ...), kind=kOutput, calls=%fused_computation.1 | convolution fusion | flops 1625554176 | bytes 14686208 | tf_op jit(solution)/shard_map/dot_general | solution.py:243
  89.9 0.0 copy-start.3
  89.9 3.3 %convert_bitcast_fusion = bf16[1,1024,1024]{2,1,0:T(8,128)(2,1)} fusion(bf16[768,1024]{1,0:T(8,128)(2,1)S(1)} %get-tuple-element.16, bf16[768,1024]{1,0:T(8,128)(2,1)S(1)} %bitcast.75, f32[768]{0:T(1024)S(1)} %mul.88), kind=kOutput, calls=%fused_computation.19 | convolution fusion | flops 1614020608 | bytes 5245952 | tf_op jit(solution)/shard_map/dot_general | solution.py:265
  93.2 3.2 %convert_bitcast_fusion.1 = bf16[1,1024,1024]{2,1,0:T(8,128)(2,1)} fusion(bf16[768,1024]{1,0:T(8,128)(2,1)S(1)} %bitcast.72, bf16[768,1024]{1,0:T(8,128)(2,1)S(1)} %get-tuple-element.22), kind=kOutput, calls=%fused_computation.20 | convolution fusion | flops 1611661312 | bytes 5242880 | tf_op jit(solution)/shard_map/dot_general | solution.py:264
  96.4 3.2 %convert_bitcast_fusion.2 = bf16[1,1024,1024]{2,1,0:T(8,128)(2,1)} fusion(bf16[768,1024]{1,0:T(8,128)(2,1)S(1)} %bitcast.73, bf16[768,1024]{1,0:T(8,128)(2,1)S(1)} %get-tuple-element.21), kind=kOutput, calls=%fused_computation.21 | convolution fusion | flops 1611661312 | bytes 5242880 | tf_op jit(solution)/shard_map/dot_general | solution.py:263
  99.5 1.8 %fusion.1 = f32[768,1024]{1,0:T(8,128)S(1)} fusion(bf16[768,1024]{1,0:T(8,128)(2,1)S(1)} %get-tuple-element.21, bf16[1,1024,1024]{2,1,0:T(8,128)(2,1)S(1)} %copy-done.9), kind=kOutput, calls=%fused_computation.9 | convolution fusion | flops 1610612736 | bytes 6815744 | tf_op jit(solution)/shard_map/dot_general | solution.py:248
  101.4 0.0 copy-start.6
  101.4 3.0 %add_convert_fusion = bf16[768,1024]{1,0:T(8,128)(2,1)} fusion(f32[768,1024]{1,0:T(8,128)S(1)} %fusion.1, bf16[768,1024]{1,0:T(8,128)(2,1)S(1)} %get-tuple-element.22, bf16[1,1024,1024]{2,1,0:T(8,128)(2,1)S(1)} %copy-done.11), kind=kOutput, calls=%fused_computation.3 | convolution fusion | flops 1612185600 | bytes 8388608 | tf_op jit(solution)/shard_map/dot_general | solution.py:248
  104.4 0.1 reshape.144
  104.5 0.7 pad.9.g
  105.2 29.1 %shard_map.112 = (bf16[16,24,1024]{2,1,0:T(8,128)(2,1)}, f32[16,8,128]{2,1,0:T(8,128)}) custom-call(bf16[2,16,24,1024]{3,2,1,0:T(8,128)(2,1)} %bitcast.69, f32[2,16,8,128]{3,2,1,0:T(8,128)} %pad.9.g), custom_call_target="tpu_custom_call" | custom-call | tf_op jit(solution)/shard_map/pallas_call | solution.py:174
  134.3 0.9 fusion.34
  135.2 0.1 reshape.149
  135.3 0.2 select_reduce_fusion.1
  135.6 0.2 copy.47
  135.7 0.3 fusion.35
  136.0 0.7 copy.46.mine
  136.7 10.8 %shard_map.113 = f32[8,128]{1,0:T(8,128)} custom-call(f32[16,8,128]{2,1,0:T(8,128)} %copy.46.mine), custom_call_target="tpu_custom_call" | custom-call | tf_op jit(solution)/shard_map/pallas_call | solution.py:174
  147.5 0.0 copy-start.7
  147.5 1.5 fusion.20
  149.0 1.3 fusion.14
  150.3 0.6 copy.56
  (26 shorter events, 0.1 us)
Async XLA Ops:
  0.6 83.0 %copy-start = (bf16[1,1024,1024]{2,1,0:T(8,128)(2,1)S(1)}, bf16[1,1024,1024]{2,1,0:T(8,128)(2,1)}, u32[]{:S(2)}) copy-start(bf16[1,1024,1024]{2,1,0:T(8,128)(2,1)} %param.13) | copy-start | bytes 6291460
  72.1 3.5 %copy-start.8 = (bf16[1,1024,1024]{2,1,0:T(8,128)(2,1)S(1)}, bf16[1,1024,1024]{2,1,0:T(8,128)(2,1)}, u32[]{:S(2)}) copy-start(bf16[1,1024,1024]{2,1,0:T(8,128)(2,1)} %param.11) | copy-start | bytes 6291460
  75.6 3.5 %copy-start.2 = (bf16[2,16,24,1024]{3,2,1,0:T(8,128)(2,1)}, bf16[2,16,24,1024]{3,2,1,0:T(8,128)(2,1)S(1)}, u32[]{:S(2)}) copy-start(bf16[2,16,24,1024]{3,2,1,0:T(8,128)(2,1)S(1)} %get-tuple-element.24) | copy-start | bytes 4718596
  75.6 3.5 %copy-start.10 = (bf16[1,1024,1024]{2,1,0:T(8,128)(2,1)S(1)}, bf16[1,1024,1024]{2,1,0:T(8,128)(2,1)}, u32[]{:S(2)}) copy-start(bf16[1,1024,1024]{2,1,0:T(8,128)(2,1)} %param.12) | copy-start | bytes 6291460
  83.7 6.2 %copy-start.4 = (bf16[2,16,24,1024]{3,2,1,0:T(8,128)(2,1)S(1)}, bf16[2,16,24,1024]{3,2,1,0:T(8,128)(2,1)}, u32[]{:S(2)}) copy-start(bf16[2,16,24,1024]{3,2,1,0:T(8,128)(2,1)} %get-tuple-element.23) | copy-start | bytes 4718596
  89.9 3.3 %copy-start.3 = (bf16[2,16,24,1024]{3,2,1,0:T(8,128)(2,1)S(1)}, bf16[2,16,24,1024]{3,2,1,0:T(8,128)(2,1)}, u32[]{:S(2)}) copy-start(bf16[2,16,24,1024]{3,2,1,0:T(8,128)(2,1)} %copy-done.2) | copy-start | bytes 4718596
  96.4 3.2 %copy-start.9 = (bf16[1,1024,1024]{2,1,0:T(8,128)(2,1)S(1)}, bf16[1,1024,1024]{2,1,0:T(8,128)(2,1)}, u32[]{:S(2)}) copy-start(bf16[1,1024,1024]{2,1,0:T(8,128)(2,1)} %param.11) | copy-start | bytes 6291460
  99.5 1.8 %copy-start.11 = (bf16[1,1024,1024]{2,1,0:T(8,128)(2,1)S(1)}, bf16[1,1024,1024]{2,1,0:T(8,128)(2,1)}, u32[]{:S(2)}) copy-start(bf16[1,1024,1024]{2,1,0:T(8,128)(2,1)} %param.12) | copy-start | bytes 6291460
  101.4 34.1 %copy-start.6 = (s32[128,2]{0,1:T(2,128)S(1)}, s32[128,2]{0,1:T(2,128)}, u32[]{:S(2)}) copy-start(s32[128,2]{0,1:T(2,128)} %param.9) | copy-start | bytes 3076
  104.4 31.1 %copy-start.1 = (bf16[128,1024]{1,0:T(8,128)(2,1)S(1)}, bf16[128,1024]{1,0:T(8,128)(2,1)}, u32[]{:S(2)}) copy-start(bf16[128,1024]{1,0:T(8,128)(2,1)} %param.7) | copy-start | bytes 786436
  105.2 43.8 %copy-start.5 = (f32[16,8,128]{2,1,0:T(8,128)S(1)}, f32[16,8,128]{2,1,0:T(8,128)}, u32[]{:S(2)}) copy-start(f32[16,8,128]{2,1,0:T(8,128)} %shard_map.110) | copy-start | bytes 196612
  147.5 2.9 %copy-start.7 = (f32[8,128]{1,0:T(8,128)S(1)}, f32[8,128]{1,0:T(8,128)}, u32[]{:S(2)}) copy-start(f32[8,128]{1,0:T(8,128)} %shard_map.113) | copy-start | bytes 12292
